TPU v7x, 256 devices: a whole 4x4x8 slice. The times are simulated.
256 devices in a mesh: replica: 16 (over y_lo, x, core), shard: 16 (over y_hi, z).
Axes of the slice: x: 4, y: 4 (y_hi: 2, y_lo: 2; y = y_hi * 2 + y_lo), z: 8, core: 2. Of those that a mesh axis runs over, the one named last changes fastest.
Arguments:
- grads: bfloat16 [16, 16, 256, 8192], P('replica', 'shard'), may hold values from -1.25 to 1.25
- master: float32 [256, 8192], P('shard'), may hold values from -0.003 to 0.003
- moment_one: float32 [256, 8192], P('shard'), may hold values from -0.75 to 0.75
- moment_two: float32 [256, 8192], P('shard'), may hold values from 0.005 to 0.2
Outputs:
- master_out: float32 [256, 8192], P('shard')
- moment_one_out: float32 [256, 8192], P('shard')
- moment_two_out: float32 [256, 8192], P('shard')
- weights: bfloat16 [256, 8192], replicated
All inputs are finite; a program needn't handle non-finite values.
Results may differ from a plain program's by a relative error of at most 0.012.
Values may be sent and summed in bfloat16 or wider, within the bound.
No kernel may reach another device: no remote copies, remote signals or barrier semaphores. Data moves between devices by JAX's collectives and lax.ppermute only.
A program may use at most 64 MiB of HBM per device.

v0:
```python
import jax
import jax.numpy as jnp
from jax import lax
from jax.sharding import PartitionSpec as P

STEP = 20


def adam_update(total, master, moment_one, moment_two):
    first = 0.9 * moment_one + 0.1 * total
    second = 0.95 * moment_two + 0.05 * total * total
    first_hat = first / (1.0 - 0.9**STEP)
    second_hat = second / (1.0 - 0.95**STEP)
    updated = master - 0.0003 * (first_hat / (jnp.sqrt(second_hat) + 1e-08) + 0.1 * master)
    return (updated, first, second)


def local(grads, master, moment_one, moment_two):
    local_grad = grads[0, 0]
    group_sum = lax.psum_scatter(
        local_grad.astype(jnp.float32).astype(jnp.bfloat16),
        "shard",
        scatter_dimension=0,
        tiled=True,
    ).astype(jnp.float32)
    total = lax.psum(group_sum, "replica")
    updated, first, second = adam_update(total, master, moment_one, moment_two)
    weights = lax.all_gather(updated.astype(jnp.bfloat16), "shard", axis=0, tiled=True)
    return (updated, first, second, weights)


def solution(mesh):
    placed = (
        P("replica", "shard", None, None),
        P("shard", None),
        P("shard", None),
        P("shard", None),
    )
    return jax.shard_map(
        local,
        mesh=mesh,
        in_specs=placed,
        out_specs=(P("shard", None), P("shard", None), P("shard", None), P()),
        check_vma=False,
    )
```

profile of v0, /device:TPU:2, one launch (start us, length us, event | category | flops | bytes accessed | tf_op | source)
XLA Modules:
  0.0 396.3 jit_solution(3998188347045665005)
XLA Ops:
  7.2 0.0 copy-start.2
  7.2 0.0 copy-start.1
  7.2 0.0 copy-start
  7.2 0.0 reduce-scatter.2.cloned.1.call-start
  7.2 0.7 reduce-scatter.2.cloned.1.call-update
  7.9 0.0 all-gather.2.cloned.1.call-start
  8.0 221.2 %reduce-scatter.2.cloned.1.call-done = bf16[16,8192]{1,0:T(8,128)(2,1)} async-done(((bf16[256,8192]{1,0:T(8,128)(2,1)}), bf16[16,8192]{1,0:T(8,128)(2,1)}) %reduce-scatter.2.cloned.1.call-update) | async-done | bytes 262160 | tf_op jit(solution)/shard_map/reduce_scatter | solution.py:20
  229.2 54.5 %all-reduce.1 = f32[16,8192]{1,0:T(8,128)S(1)} all-reduce(bf16[16,8192]{1,0:T(8,128)(2,1)} %reduce-scatter.2.cloned.1.call-done), channel_id=1, replica_groups=mesh['replica'=16,'shard'=16] {'replica'}, use_global_device_ids=true, to_apply=%region_1.0 | all-reduce | flops 131072 | bytes 786432 | tf_op jit(solution)/shard_map/psum | solution.py:26
  283.7 0.0 copy-done.2
  283.7 0.0 copy-done.1
  283.7 0.0 copy-done
  283.7 1.5 fusion.1
  285.2 0.0 all-gather.2.cloned.1.call-update
  285.2 99.6 %all-gather.2.cloned.1.call-done = bf16[256,8192]{1,0:T(8,128)(2,1)} async-done(((bf16[16,8192]{1,0:T(8,128)(2,1)}), bf16[256,8192]{1,0:T(8,128)(2,1)}) %all-gather.2.cloned.1.call-update) | async-done | bytes 4194320 | tf_op jit(solution)/shard_map/all_gather | solution.py:28
  384.8 4.6 %copy.11 = bf16[256,8192]{1,0:T(8,128)(2,1)} copy(bf16[256,8192]{1,0:T(8,128)(2,1)} %all-gather.2.cloned.1.call-done) | data formatting | bytes 8388608
Async XLA Ops:
  7.2 276.5 %copy-start.2 = (f32[16,8192]{1,0:T(8,128)S(1)}, f32[16,8192]{1,0:T(8,128)}, u32[]{:S(2)}) copy-start(f32[16,8192]{1,0:T(8,128)} %param.7) | copy-start | bytes 1572868
  7.2 276.5 %copy-start.1 = (f32[16,8192]{1,0:T(8,128)S(1)}, f32[16,8192]{1,0:T(8,128)}, u32[]{:S(2)}) copy-start(f32[16,8192]{1,0:T(8,128)} %param.6) | copy-start | bytes 1572868
  7.2 276.5 %copy-start = (f32[16,8192]{1,0:T(8,128)S(1)}, f32[16,8192]{1,0:T(8,128)}, u32[]{:S(2)}) copy-start(f32[16,8192]{1,0:T(8,128)} %param.5) | copy-start | bytes 1572868
  7.2 222.0 %reduce-scatter.2.cloned.1.call-start = ((), (), s32[]{:S(2)}) async-start(), calls=%async_computation.1 | async-start | bytes 4456448 | tf_op jit(solution)/shard_map/reduce_scatter | solution.py:20
  7.9 376.8 %all-gather.2.cloned.1.call-start = ((), (), s32[]{:S(2)}) async-start(), calls=%async_computation.2 | async-start | bytes 4456448 | tf_op jit(solution)/shard_map/all_gather | solution.py:28
Sparse Core Ops, SparseCore 0:
  12.0 217.1 reduce-scatter.1
  285.3 99.4 all-gather.1
where the time goes:
time: 397 us; the launch traced here: 396 us
  waiting for transfers between devices  321 us (81%)
  blocking collectives  54.5 us (14%)
  between operations  14.1 us (4%)
  local copies, waits for them, and re-layouts  4.65 us (1%)
    reduce_scatter x1, waiting for transfers between devices, local(): lax.psum_scatter(local_grad.astype(jnp.float32).astype(jnp.bfloat16), 'sh...  221 us
    all_gather x1, waiting for transfers between devices, local(): lax.all_gather(updated.astype(jnp.bfloat16), 'shard', axis=0, tiled=True)  99.6 us
    psum x1, blocking collectives, local(): total = lax.psum(group_sum, 'replica')  54.5 us
  transfers between devices with their start and end apart: 2, of which 2 were waited for; matrix products, arithmetic and copies ran while one was open for 0% of the time, Pallas kernels for 0%

commit v1 on v0

--- a/solution.py
+++ b/solution.py
@@ -23,7 +23,7 @@
         scatter_dimension=0,
         tiled=True,
     ).astype(jnp.float32)
-    total = lax.psum(group_sum, "replica")
+    total = jnp.sum(jax.lax.all_gather(group_sum, "replica"), axis=0)
     updated, first, second = adam_update(total, master, moment_one, moment_two)
     weights = lax.all_gather(updated.astype(jnp.bfloat16), "shard", axis=0, tiled=True)
     return (updated, first, second, weights)

time: 397 us -> 402 us (1.013)
  waiting for transfers between devices: 321 us -> 376 us
  blocking collectives: 54.5 us -> 0 us
  other arithmetic: 1.47 us -> 7.18 us
    psum x1 -> x0, blocking collectives: 54.5 us -> none  [local(): total = lax.psum(group_sum, 'replica')]
    all_gather x0 -> x1, waiting for transfers between devices: none -> 53 us  [local(): total = jnp.sum(jax.lax.all_gather(group_sum, 'replica'), axis=0)]
  transfers between devices with their start and end apart: 2 -> 3, of which waited for: 2 -> 3; matrix products, arithmetic and copies ran while one was open for 0% -> 0% of each run, Pallas kernels for 0% -> 0%
where the time goes in v1:
time: 402 us
  waiting for transfers between devices  376 us (94%)
  between operations  13.8 us (3%)
  other arithmetic  7.18 us (2%)
  local copies, waits for them, and re-layouts  4.65 us (1%)
    reduce_scatter x1, waiting for transfers between devices, local(): lax.psum_scatter(local_grad.astype(jnp.float32).astype(jnp.bfloat16), 'sh...  221 us
    all_gather x1, waiting for transfers between devices, local(): lax.all_gather(updated.astype(jnp.bfloat16), 'shard', axis=0, tiled=True)  101 us
    all_gather x1, waiting for transfers between devices, local(): total = jnp.sum(jax.lax.all_gather(group_sum, 'replica'), axis=0)  53 us
  transfers between devices with their start and end apart: 3, of which 3 were waited for; matrix products, arithmetic and copies ran while one was open for 0% of the time, Pallas kernels for 0%

profile of v1, /device:TPU:2, one launch (start us, length us, event | category | flops | bytes accessed | tf_op | source)
XLA Modules:
  0.0 401.6 jit_solution(6137524616271892713)
XLA Ops:
  7.2 0.0 reduce-scatter.2.cloned.1.call-start
  7.2 0.7 reduce-scatter.2.cloned.1.call-update
  7.9 0.0 all-gather.6.cloned.1.call-start
  7.9 221.2 %reduce-scatter.2.cloned.1.call-done = bf16[16,8192]{1,0:T(8,128)(2,1)} async-done(((bf16[256,8192]{1,0:T(8,128)(2,1)}), bf16[16,8192]{1,0:T(8,128)(2,1)}) %reduce-scatter.2.cloned.1.call-update) | async-done | bytes 262160 | tf_op jit(solution)/shard_map/reduce_scatter | solution.py:20
  229.2 1.8 all_gather.16
  230.9 0.0 all-gather.6.cloned.1.call-update
  231.0 0.0 all-gather.4.cloned.1.call-start
  231.0 53.0 %all-gather.6.cloned.1.call-done = f32[256,8192]{1,0:T(8,128)} async-done(((f32[16,8192]{1,0:T(8,128)}), f32[256,8192]{1,0:T(8,128)}) %all-gather.6.cloned.1.call-update) | async-done | bytes 8388624 | tf_op jit(solution)/shard_map/all_gather | solution.py:26
  284.0 0.0 copy-start
  284.0 0.0 copy-start.1
  284.0 0.0 copy-start.2
  284.0 3.9 reduce_sum.9
  288.0 0.0 copy-done
  288.0 0.0 copy-done.1
  288.0 0.0 copy-done.2
  288.0 1.5 fusion.1
  289.5 0.0 all-gather.4.cloned.1.call-update
  289.5 100.9 %all-gather.4.cloned.1.call-done = bf16[256,8192]{1,0:T(8,128)(2,1)} async-done(((bf16[16,8192]{1,0:T(8,128)(2,1)}), bf16[256,8192]{1,0:T(8,128)(2,1)}) %all-gather.4.cloned.1.call-update) | async-done | bytes 4194320 | tf_op jit(solution)/shard_map/all_gather | solution.py:28
  390.4 4.6 %copy.9 = bf16[256,8192]{1,0:T(8,128)(2,1)} copy(bf16[256,8192]{1,0:T(8,128)(2,1)} %all-gather.4.cloned.1.call-done) | data formatting | bytes 8388608
Async XLA Ops:
  7.2 222.0 %reduce-scatter.2.cloned.1.call-start = ((), (), s32[]{:S(2)}) async-start(), calls=%async_computation.1 | async-start | bytes 4456448 | tf_op jit(solution)/shard_map/reduce_scatter | solution.py:20
  7.9 276.1 %all-gather.6.cloned.1.call-start = ((), (), s32[]{:S(2)}) async-start(), calls=%async_computation.3 | async-start | bytes 8912896 | tf_op jit(solution)/shard_map/all_gather | solution.py:26
  231.0 159.5 %all-gather.4.cloned.1.call-start = ((), (), s32[]{:S(2)}) async-start(), calls=%async_computation.2 | async-start | bytes 4456448 | tf_op jit(solution)/shard_map/all_gather | solution.py:28
  284.0 3.9 copy-start
  284.0 4.0 copy-start.1
  284.0 4.0 copy-start.2
Sparse Core Ops, SparseCore 0:
  12.0 217.1 reduce-scatter.1
  231.6 52.4 all-gather.5
  289.6 100.7 all-gather.3
